TPU v7x, 32 devices: a whole 2x2x4 slice. The times are simulated.
32 devices in a mesh: dp: 8 (over z, x), tp: 4 (over y, core).
Axes of the slice: x: 2, y: 2, z: 4, core: 2. Of those that a mesh axis runs over, the one named last changes fastest.
Arguments:
- activations: bfloat16 [2048, 4096], P('dp'), may hold values from -6 to 6
- out_grads: bfloat16 [2048, 4096], P('dp', 'tp'), may hold values from -6 to 6
- residual: bfloat16 [32768, 4096], P('dp', 'tp'), may hold values from -24 to 24
- right_prev: bfloat16 [4096, 32], P('tp'), may hold values from -6 to 6
Outputs:
- update: bfloat16 [4096, 4096], P(None, 'tp')
- left_basis: float32 [4096, 32], replicated
- right_factor: float32 [4096, 32], P('tp')
All inputs are finite; a program needn't handle non-finite values.
Results may differ from a plain program's by a relative error of at most 0.0061.
Values sent between devices are 32-bit elements; how exact they have to be, the bound alone decides.
A program may use at most 64 MiB of HBM per device.

v0:
```python
import jax
import jax.numpy as jnp
from jax import lax
from jax.sharding import PartitionSpec as P


def shards(activations, out_grads, residual, right_prev):
    product = lax.dot_general(
        activations, out_grads, (((0,), (0,)), ((), ())), preferred_element_type=jnp.float32
    )
    merged = (product + residual.astype(jnp.float32)).astype(jnp.bfloat16)
    shard_sum = lax.psum_scatter(
        jnp.dot(merged, right_prev, preferred_element_type=jnp.float32),
        "tp",
        scatter_dimension=0,
        tiled=True,
    )
    block_sum = lax.psum(shard_sum, "dp")
    block_gram = jnp.dot(block_sum.T, block_sum, precision=lax.Precision.HIGHEST)
    gram_matrix = lax.psum(block_gram, "tp")
    lower_factor = jnp.linalg.cholesky(gram_matrix)
    basis_block = lax.linalg.triangular_solve(
        lower_factor, block_sum, left_side=False, lower=True, transpose_a=True
    )
    left_basis = lax.all_gather(basis_block, "tp", axis=0, tiled=True)
    left_half = left_basis.astype(jnp.bfloat16)
    coeff_terms = lax.dot_general(
        merged, left_half, (((0,), (0,)), ((), ())), preferred_element_type=jnp.float32
    )
    right_factor = lax.psum(coeff_terms, "dp") / lax.axis_size("dp")
    update = jnp.dot(left_basis, right_factor.T, precision=lax.Precision.HIGHEST).astype(
        jnp.bfloat16
    )
    return (update, left_basis, right_factor)


def solution(mesh):
    in_specs = (P("dp", None), P("dp", "tp"), P("dp", "tp"), P("tp", None))
    out_specs = (P(None, "tp"), P(), P("tp", None))
    return jax.shard_map(shards, mesh=mesh, in_specs=in_specs, out_specs=out_specs, check_vma=False)
```

profile of v0, /device:TPU:0, one launch (start us, length us, event | category | flops | bytes accessed | tf_op | source)
XLA Modules:
  0.0 244.7 jit_solution(3257671253548092697)
XLA Ops:
  7.2 0.0 reduce-scatter.2.cloned.1.call-start
  7.2 1.5 copy-done
  8.8 6.0 %add_convert_fusion = bf16[4096,1024]{1,0:T(8,128)(2,1)S(1)} fusion(bf16[4096,1024]{1,0:T(8,128)(2,1)} %param.6, bf16[256,4096]{1,0:T(8,128)(2,1)S(1)} %copy-done, bf16[256,1024]{1,0:T(8,128)(2,1)} %param.5), kind=kOutput, calls=%fused_computation | convolution fusion | flops 2160066560 | bytes 19398656 | tf_op jit(solution)/shard_map/dot_general | solution.py:8
  14.7 3.4 %copy-done.1 = bf16[4096,1024]{1,0:T(8,128)(2,1)} copy-done((bf16[4096,1024]{1,0:T(8,128)(2,1)}, bf16[4096,1024]{1,0:T(8,128)(2,1)S(1)}, u32[]{:S(2)}) %copy-start.1) | copy-done | bytes 8388632
  18.1 3.4 %fusion.6 = f32[4096,32]{0,1:T(8,128)} fusion(bf16[4096,1024]{1,0:T(8,128)(2,1)S(1)} %add_convert_fusion, bf16[1024,32]{0,1:T(8,128)(2,1)S(1)} %copy-done.3), kind=kOutput, calls=%fused_computation.15 | convolution fusion | flops 268435456 | bytes 8978432 | tf_op jit(solution)/shard_map/dot_general | solution.py:13
  21.5 0.0 reduce-scatter.2.cloned.1.call-update
  21.5 0.0 all-reduce.3.cloned.1.call-start
  21.6 24.5 %reduce-scatter.2.cloned.1.call-done = f32[1024,32]{0,1:T(8,128)} async-done(((f32[4096,32]{0,1:T(8,128)}), f32[1024,32]{0,1:T(8,128)}) %reduce-scatter.2.cloned.1.call-update) | async-done | bytes 131088 | tf_op jit(solution)/shard_map/reduce_scatter | solution.py:12
  46.1 0.0 all-reduce.5.cloned.1.call-start
  46.1 73.8 %all-reduce.3.cloned.1.call-done = f32[1024,32]{0,1:T(8,128)} async-done(((f32[1024,32]{0,1:T(8,128)}), f32[1024,32]{0,1:T(8,128)}) %all-reduce.3.cloned.1.call-update) | async-done | bytes 131088 | tf_op jit(solution)/shard_map/psum | solution.py:18
  119.9 1.2 fusion.7
  121.1 10.1 %psum.22 = f32[32,32]{0,1:T(8,128)S(1)} all-reduce(f32[32,32]{0,1:T(8,128)S(1)} %fusion.7), channel_id=1, replica_groups=mesh['dp'=8,'tp'=4] {'tp'}, use_global_device_ids=true, to_apply=%region_2.0 | all-reduce | flops 1024 | bytes 8192 | tf_op jit(solution)/shard_map/psum | solution.py:20
  131.3 0.1 copy.8
  131.3 2.9 %cholesky.16 = f32[32,32]{1,0:T(8,128)S(1)} custom-call(f32[32,32]{1,0:T(8,128)S(1)} %fusion.5), custom_call_target="Cholesky" | custom-call | tf_op jit(solution)/shard_map/jit(cholesky)/cholesky | solution.py:21
  134.3 0.6 compare_reduce_fusion
  134.9 0.7 fusion.2
  135.6 2.4 custom-call.6
  138.0 1.2 fusion.3
  139.3 7.3 %all_gather.3 = f32[4096,32]{0,1:T(8,128)S(1)} all-gather(f32[1024,32]{0,1:T(8,128)S(1)} %fusion.3), channel_id=1, replica_groups=mesh['dp'=8,'tp'=4] {'tp'}, dimensions={0}, use_global_device_ids=true | all-gather | bytes 655360 | tf_op jit(solution)/shard_map/all_gather | solution.py:25
  146.6 5.6 %fusion = f32[1024,32]{0,1:T(8,128)} fusion(bf16[4096,1024]{1,0:T(8,128)(2,1)} %copy-done.1, f32[4096,32]{0,1:T(8,128)S(1)} %all_gather.3), kind=kOutput, calls=%fused_computation.2 | convolution fusion | flops 268566528 | bytes 9043968 | tf_op jit(solution)/shard_map/dot_general | solution.py:27
  152.2 69.1 %all-reduce.5.cloned.1.call-done = f32[1024,32]{0,1:T(8,128)} async-done(((f32[1024,32]{0,1:T(8,128)}), f32[1024,32]{0,1:T(8,128)}) %all-reduce.5.cloned.1.call-update) | async-done | bytes 131088 | tf_op jit(solution)/shard_map/psum | solution.py:30
  221.2 0.9 broadcast_multiply_fusion
  222.1 15.3 %convolution_convert_fusion = bf16[4096,1024]{1,0:T(8,128)(2,1)} fusion(f32[4096,32]{0,1:T(8,128)S(1)} %all_gather.3, f32[1024,32]{0,1:T(8,128)S(1)} %broadcast_multiply_fusion), kind=kOutput, calls=%fused_computation.1 | convolution fusion | flops 1614807040 | bytes 9043968 | tf_op jit(solution)/shard_map/dot_general | solution.py:31
  237.4 0.8 copy.13
  (10 shorter events, 0.1 us)
Async XLA Ops:
  7.2 1.6 copy-start
  7.2 10.9 %copy-start.3 = (bf16[1024,32]{0,1:T(8,128)(2,1)S(1)}, bf16[1024,32]{0,1:T(8,128)(2,1)}, u32[]{:S(2)}) copy-start(bf16[1024,32]{0,1:T(8,128)(2,1)} %param.7) | copy-start | bytes 196612
  7.2 38.8 %reduce-scatter.2.cloned.1.call-start = ((), (), s32[]{:S(2)}) async-start(), calls=%async_computation.1 | async-start | bytes 655360 | tf_op jit(solution)/shard_map/reduce_scatter | solution.py:12
  14.7 3.4 %copy-start.1 = (bf16[4096,1024]{1,0:T(8,128)(2,1)}, bf16[4096,1024]{1,0:T(8,128)(2,1)S(1)}, u32[]{:S(2)}) copy-start(bf16[4096,1024]{1,0:T(8,128)(2,1)S(1)} %add_convert_fusion) | copy-start | bytes 25165828
  21.5 98.4 %all-reduce.3.cloned.1.call-start = ((), (), s32[]{:S(2)}) async-start(), calls=%async_computation.2 | async-start | bytes 262144 | tf_op jit(solution)/shard_map/psum | solution.py:18
  46.1 175.2 %all-reduce.5.cloned.1.call-start = ((), (), s32[]{:S(2)}) async-start(), calls=%async_computation.3 | async-start | bytes 262144 | tf_op jit(solution)/shard_map/psum | solution.py:30
  222.1 16.1 %copy-start.2 = (f32[1024,32]{0,1:T(8,128)}, f32[1024,32]{0,1:T(8,128)S(1)}, u32[]{:S(2)}) copy-start(f32[1024,32]{0,1:T(8,128)S(1)} %broadcast_multiply_fusion) | copy-start | bytes 393220
Sparse Core Ops, SparseCore 0:
  21.6 24.3 reduce-scatter.1
  49.4 70.4 all-reduce.2
  152.3 68.8 all-reduce.4
where the time goes:
time: 245 us
  waiting for transfers between devices  167 us (68%)
  matrix products  32.6 us (13%)
  blocking collectives  17.4 us (7%)
  between operations  13.8 us (6%)
  other arithmetic  7.6 us (3%)
  local copies, waits for them, and re-layouts  5.8 us (2%)
    psum x1, waiting for transfers between devices, shards(): block_sum = lax.psum(shard_sum, 'dp')  73.8 us
    psum x1, waiting for transfers between devices, shards(): right_factor = lax.psum(coeff_terms, 'dp') / lax.axis_size('dp')  69.1 us
    reduce_scatter x1, waiting for transfers between devices, shards(): lax.psum_scatter(jnp.dot(merged, right_prev, preferred_element_type=jnp.f...  24.5 us
    dot_general x1, matrix products, shards(): jnp.dot(left_basis, right_factor.T, precision=lax.Precision.HIGHEST)  15.3 us
    psum x1, blocking collectives, shards(): gram_matrix = lax.psum(block_gram, 'tp')  10.1 us
    all_gather x1, blocking collectives, shards(): left_basis = lax.all_gather(basis_block, 'tp', axis=0, tiled=True)  7.28 us
    dot_general x1, matrix products, shards(): lax.dot_general(activations, out_grads, (((0,), (0,)), ((), ())), preferr...  5.95 us
    unnamed x9, local copies, waits for them, and re-layouts  5.73 us
  transfers between devices with their start and end apart: 3, of which 3 were waited for; matrix products, arithmetic and copies ran while one was open for 0% of the time, Pallas kernels for 0%

commit v1 on v0

v1 whole, which is shorter than its diff:
```python
import functools
import itertools

import jax
import jax.numpy as jnp
from jax import lax
from jax.experimental import pallas as pl
from jax.experimental.pallas import tpu as pltpu
from jax.sharding import PartitionSpec as P

LANES = 128
HIGHEST = lax.Precision.HIGHEST


def plain_shards(activations, out_grads, residual, right_prev):
    product = lax.dot_general(
        activations, out_grads, (((0,), (0,)), ((), ())), preferred_element_type=jnp.float32
    )
    merged = (product + residual.astype(jnp.float32)).astype(jnp.bfloat16)
    shard_sum = lax.psum_scatter(
        jnp.dot(merged, right_prev, preferred_element_type=jnp.float32),
        "tp",
        scatter_dimension=0,
        tiled=True,
    )
    block_sum = lax.psum(shard_sum, "dp")
    block_gram = jnp.dot(block_sum.T, block_sum, precision=HIGHEST)
    gram_matrix = lax.psum(block_gram, "tp")
    lower_factor = jnp.linalg.cholesky(gram_matrix)
    basis_block = lax.linalg.triangular_solve(
        lower_factor, block_sum, left_side=False, lower=True, transpose_a=True
    )
    left_basis = lax.all_gather(basis_block, "tp", axis=0, tiled=True)
    left_half = left_basis.astype(jnp.bfloat16)
    coeff_terms = lax.dot_general(
        merged, left_half, (((0,), (0,)), ((), ())), preferred_element_type=jnp.float32
    )
    right_factor = lax.psum(coeff_terms, "dp") / lax.axis_size("dp")
    update = jnp.dot(left_basis, right_factor.T, precision=HIGHEST).astype(jnp.bfloat16)
    return (update, left_basis, right_factor)


def digits_of(axis, size):
    if size == 1:
        return []
    if size % 2 == 0 and size > 2:
        return [(axis, 1, 2), (axis, 2, size // 2)]
    return [(axis, 1, size)]


def members(stage):
    count = 1
    for _, _, size in stage:
        count *= size
    return count


def offsets(stage):
    return list(itertools.product(*[range(size) for _, _, size in stage]))[1:]


def member_index(stage, place):
    index = 0
    for axis, stride, size in stage:
        index = index * size + (place[axis] // stride) % size
    return index


def moved(stage, offset, place, sign=1):
    there = dict(place)
    for (axis, stride, size), step in zip(stage, offset):
        digit = (place[axis] // stride) % size
        there[axis] = there[axis] + (((digit + sign * step + size) % size) - digit) * stride
    return there


def round_kernel(
    left_stages, right_stages, n_chunk, axes,
    act, grads, resid, right_prev, basis_out, coeff_out,
    xbuf, ybuf, merged, acc, full, acc2, full2, *rest,
):
    n_left = len(left_stages)
    left_recv = rest[:n_left]
    right_recv = rest[n_left : n_left + len(right_stages)]
    in_sem, send_sem, recv_sem = rest[n_left + len(right_stages) :]
    place = {axis: lax.axis_index(axis) for axis in axes}
    barrier = pltpu.get_barrier_semaphore()
    peers = {}
    for stage in left_stages + right_stages:
        for offset in offsets(stage):
            key = tuple(sorted((d, s) for d, s in zip(stage, offset) if s))
            peers[key] = moved(stage, offset, place)
    for peer in peers.values():
        pl.semaphore_signal(barrier, inc=1, device_id=peer, device_id_type=pl.DeviceIdType.MESH)

    rows = resid.shape[0]
    chunk = rows // n_chunk
    per = chunk // LANES
    width = acc.shape[1]

    def x_copy(c):
        at = pl.multiple_of(c * chunk, chunk)
        return pltpu.make_async_copy(act.at[:, pl.ds(at, chunk)], xbuf.at[c], in_sem.at[c])

    def e_copy(c):
        at = pl.multiple_of(c * chunk, chunk)
        return pltpu.make_async_copy(
            resid.at[pl.ds(at, chunk), :], merged.at[pl.ds(at, chunk), :], in_sem.at[n_chunk + c]
        )

    y_copy = pltpu.make_async_copy(grads, ybuf, in_sem.at[2 * n_chunk])
    y_copy.start()
    for c in range(n_chunk):
        x_copy(c).start()
        e_copy(c).start()
    y_copy.wait()

    def merge(c, carry):
        x_copy(c).wait()
        e_copy(c).wait()
        at = pl.multiple_of(c * chunk, chunk)
        product = lax.dot_general(
            xbuf[c], ybuf[...], (((0,), (0,)), ((), ())), preferred_element_type=jnp.float32
        )
        piece = (product + merged[pl.ds(at, chunk), :].astype(jnp.float32)).astype(jnp.bfloat16)
        merged[pl.ds(at, chunk), :] = piece
        term = lax.dot_general(
            right_prev[...], piece, (((1,), (1,)), ((), ())), preferred_element_type=jnp.float32
        )
        for b in range(per):
            acc[c * per + b] = term[:, b * LANES : (b + 1) * LANES]
        return carry

    lax.fori_loop(0, n_chunk, merge, 0)
    pl.semaphore_wait(barrier, len(peers))

    slot = [0]

    def remote(src, dst, peer):
        n = slot[0]
        slot[0] += 1
        return pltpu.make_async_remote_copy(
            src_ref=src, dst_ref=dst, send_sem=send_sem.at[n], recv_sem=recv_sem.at[n],
            device_id=peer, device_id_type=pl.DeviceIdType.MESH,
        )

    def all_reduce(stages, acc_ref, recv_refs, full_ref):
        lo, count = 0, acc_ref.shape[0]
        held, sent = [], []
        for stage, recv in zip(stages, recv_refs):
            size = count // members(stage)
            copies = []
            for k, offset in enumerate(offsets(stage)):
                peer = moved(stage, offset, place)
                start = lo + member_index(stage, peer) * size
                copies.append(remote(acc_ref.at[pl.ds(start, size)], recv.at[k], peer))
                copies[-1].start()
            held.append((lo, count))
            lo, count = lo + member_index(stage, place) * size, size
            total = acc_ref[pl.ds(lo, count)]
            for k, copy in enumerate(copies):
                copy.wait_recv()
                total = total + recv[k]
            sent += copies
            if stage is stages[-1]:
                full_ref[pl.ds(lo, count)] = total
            else:
                acc_ref[pl.ds(lo, count)] = total
        for stage, (outer, outer_count) in zip(reversed(stages), reversed(held)):
            copies = []
            for offset in offsets(stage):
                peer = moved(stage, offset, place)
                mine = full_ref.at[pl.ds(lo, count)]
                copies.append(remote(mine, mine, peer))
                copies[-1].start()
            for copy in copies:
                copy.wait_recv()
            sent += copies
            lo, count = outer, outer_count
        return sent

    sent = all_reduce(left_stages, acc, left_recv, full)
    left_sum = jnp.concatenate([full[b] for b in range(full.shape[0])], axis=1)
    gram = lax.dot_general(
        left_sum, left_sum, (((1,), (1,)), ((), ())),
        precision=HIGHEST, preferred_element_type=jnp.float32,
    )
    row_id = lax.broadcasted_iota(jnp.int32, (width, LANES), 0)
    col_id = lax.broadcasted_iota(jnp.int32, (width, LANES), 1)
    work = jnp.concatenate(
        [gram, (row_id + width == col_id).astype(jnp.float32)[:, width:]], axis=1
    )
    for j in range(width):
        column = jnp.broadcast_to(work[:, j : j + 1], (width, LANES))
        scaled = work[j : j + 1, :] / column[j : j + 1, :]
        work = work - jnp.where(row_id > j, column, 0.0) * scaled
    pivots = jnp.sum(jnp.where(row_id == col_id, work, 0.0), axis=1, keepdims=True)
    inverse = work[:, width : 2 * width] / jnp.sqrt(pivots)
    basis = jnp.dot(inverse, left_sum, precision=HIGHEST, preferred_element_type=jnp.float32)
    basis_out[...] = basis
    half = basis.astype(jnp.bfloat16)
    columns = merged.shape[1]
    tile = 2 * LANES

    def terms(j, carry):
        at = pl.multiple_of(j * tile, tile)
        part = jnp.dot(half, merged[:, pl.ds(at, tile)], preferred_element_type=jnp.float32)
        acc2[2 * j] = part[:, :LANES]
        acc2[2 * j + 1] = part[:, LANES:]
        return carry

    lax.fori_loop(0, columns // tile, terms, 0)
    sent += all_reduce(right_stages, acc2, right_recv, full2)
    scale = 1.0 / members(right_stages[0])
    for b in range(full2.shape[0]):
        coeff_out[:, b * LANES : (b + 1) * LANES] = full2[b] * scale
    for copy in sent:
        copy.wait_send()


def split(value):
    high = value.astype(jnp.bfloat16)
    return high, (value - high.astype(jnp.float32)).astype(jnp.bfloat16)


def update_kernel(basis, coeff, update_out, basis_out, coeff_out):
    left_high, left_low = split(basis[...])
    right_high, right_low = split(coeff[...])
    left = jnp.concatenate([left_high, left_low, left_high], axis=0)
    right = jnp.concatenate([right_high, right_high, right_low], axis=0)
    update_out[...] = lax.dot_general(
        left, right, (((0,), (0,)), ((), ())), preferred_element_type=jnp.float32
    ).astype(jnp.bfloat16)
    basis_out[...] = basis[...]
    coeff_out[...] = coeff[...]


def fast_shards(axes, sizes, activations, out_grads, residual, right_prev):
    rows, columns = residual.shape
    tokens = activations.shape[0]
    rank = right_prev.shape[1]
    n_dp, n_tp = sizes["dp"], sizes["tp"]
    tp_digits, dp_digits = digits_of("tp", n_tp), digits_of("dp", n_dp)
    left_stages = [s for s in (tp_digits[:1], tp_digits[1:] + dp_digits[:1], dp_digits[1:]) if s]
    right_stages = [dp_digits]
    n_chunk = max(1, rows // 512)
    blocks, blocks2 = rows // LANES, columns // LANES

    def recv_shapes(stages, count):
        shapes = []
        for stage in stages:
            count //= members(stage)
            shapes.append(pltpu.VMEM((members(stage) - 1, count, rank, LANES), jnp.float32))
        return shapes

    n_copies = 2 * sum(members(s) - 1 for s in left_stages + right_stages)
    vmem = pl.BlockSpec(memory_space=pltpu.VMEM)
    hbm = pl.BlockSpec(memory_space=pl.ANY)
    basis, coeff = pl.pallas_call(
        functools.partial(round_kernel, left_stages, right_stages, n_chunk, axes),
        out_shape=(
            jax.ShapeDtypeStruct((rank, rows), jnp.float32),
            jax.ShapeDtypeStruct((rank, columns), jnp.float32),
        ),
        in_specs=[hbm, hbm, hbm, vmem],
        out_specs=(vmem, vmem),
        scratch_shapes=[
            pltpu.VMEM((n_chunk, tokens, rows // n_chunk), jnp.bfloat16),
            pltpu.VMEM((tokens, columns), jnp.bfloat16),
            pltpu.VMEM((rows, columns), jnp.bfloat16),
            pltpu.VMEM((blocks, rank, LANES), jnp.float32),
            pltpu.VMEM((blocks, rank, LANES), jnp.float32),
            pltpu.VMEM((blocks2, rank, LANES), jnp.float32),
            pltpu.VMEM((blocks2, rank, LANES), jnp.float32),
            *recv_shapes(left_stages, blocks),
            *recv_shapes(right_stages, blocks2),
            pltpu.SemaphoreType.DMA((2 * n_chunk + 1,)),
            pltpu.SemaphoreType.DMA((n_copies,)),
            pltpu.SemaphoreType.DMA((n_copies,)),
        ],
        compiler_params=pltpu.CompilerParams(
            collective_id=0, has_side_effects=True, vmem_limit_bytes=40 * 2**20
        ),
        name="powersgd_round",
    )(activations, out_grads, residual, right_prev.T)
    step = min(rows, 512)
    update, basis, coeff = pl.pallas_call(
        update_kernel,
        grid=(rows // step,),
        out_shape=(
            jax.ShapeDtypeStruct((rows, columns), jnp.bfloat16),
            jax.ShapeDtypeStruct((rank, rows), jnp.float32),
            jax.ShapeDtypeStruct((rank, columns), jnp.float32),
        ),
        in_specs=[
            pl.BlockSpec((rank, step), lambda i: (0, i)),
            pl.BlockSpec((rank, columns), lambda i: (0, 0)),
        ],
        out_specs=(
            pl.BlockSpec((step, columns), lambda i: (i, 0)),
            pl.BlockSpec((rank, step), lambda i: (0, i)),
            pl.BlockSpec((rank, columns), lambda i: (0, 0)),
        ),
        compiler_params=pltpu.CompilerParams(vmem_limit_bytes=16 * 2**20),
        name="powersgd_update",
    )(basis, coeff)
    return update, basis.T, coeff.T


def shards(axes, sizes, activations, out_grads, residual, right_prev):
    rows, columns = residual.shape
    n_dp, n_tp = sizes["dp"], sizes["tp"]
    fits = (
        rows % (LANES * n_dp * n_tp) == 0
        and rows % 512 == 0
        and columns % (2 * LANES) == 0
        and columns % (LANES * n_dp) == 0
        and right_prev.shape[1] * 2 <= LANES
        and n_dp > 1
    )
    if not fits:
        return plain_shards(activations, out_grads, residual, right_prev)
    return fast_shards(axes, sizes, activations, out_grads, residual, right_prev)


def solution(mesh):
    in_specs = (P("dp", None), P("dp", "tp"), P("dp", "tp"), P("tp", None))
    out_specs = (P(None, "tp"), P(), P("tp", None))
    body = functools.partial(shards, mesh.axis_names, dict(mesh.shape))
    return jax.shard_map(body, mesh=mesh, in_specs=in_specs, out_specs=out_specs, check_vma=False)
```

time: 245 us -> 59.7 us (0.24)
  waiting for transfers between devices: 167 us -> 0 us
  Pallas kernels: 0 us -> 51.9 us
  matrix products: 32.6 us -> 0 us
  blocking collectives: 17.4 us -> 0 us
  between operations: 13.8 us -> 0.65 us
  other arithmetic: 7.6 us -> 0 us
    psum x2 -> x0, waiting for transfers between devices: 143 us -> none  [the longest x1 73.8 us: shards(): block_sum = lax.psum(shard_sum, 'dp')]
    pallas_call x0 -> x2, Pallas kernels: none -> 51.9 us  [the longest x1 45.7 us: fast_shards(): pl.pallas_call(functools.partial(round_kernel, left_stages, right_stages,...]
    dot_general x5 -> x0, matrix products: 31.4 us -> none  [the longest x1 15.3 us: shards(): jnp.dot(left_basis, right_factor.T, precision=lax.Precision.HIGHEST)]
    reduce_scatter x1 -> x0, waiting for transfers between devices: 24.5 us -> none  [shards(): lax.psum_scatter(jnp.dot(merged, right_prev, preferred_element_type=jnp.f...]
    psum x1 -> x0, blocking collectives: 10.1 us -> none  [shards(): gram_matrix = lax.psum(block_gram, 'tp')]
    all_gather x1 -> x0, blocking collectives: 7.28 us -> none  [shards(): left_basis = lax.all_gather(basis_block, 'tp', axis=0, tiled=True)]
    another operation x5 -> x0, other arithmetic: 6.68 us -> none  [the longest x3 3.59 us: shards(): lower_factor = jnp.linalg.cholesky(gram_matrix)]
    unnamed x9 -> x8, local copies, waits for them, and re-layouts: 5.73 us -> 6.85 us
  transfers between devices with their start and end apart: 3 -> 0, of which waited for: 3 -> 0; matrix products, arithmetic and copies ran while one was open for 0% -> 0% of each run, Pallas kernels for 0% -> 0%
where the time goes in v1:
time: 59.7 us; the launch traced here: 59.4 us
  Pallas kernels  51.9 us (87%)
  local copies, waits for them, and re-layouts  6.85 us (11%)
  between operations  0.65 us (1%)
    pallas_call x1, Pallas kernels, fast_shards(): pl.pallas_call(functools.partial(round_kernel, left_stages, right_stages,...  45.7 us
    unnamed x8, local copies, waits for them, and re-layouts  6.85 us
    pallas_call x1, Pallas kernels, fast_shards(): pl.pallas_call(update_kernel, grid=(rows // step,), out_shape=(jax.ShapeD...  6.25 us

profile of v1, /device:TPU:0, one launch (start us, length us, event | category | flops | bytes accessed | tf_op | source)
XLA Modules:
  0.0 59.4 jit_solution(11023517840153112107)
XLA Ops:
  0.6 0.0 copy-start
  0.6 3.4 %copy-done = bf16[4096,1024]{1,0:T(8,128)(2,1)S(1)} copy-done((bf16[4096,1024]{1,0:T(8,128)(2,1)S(1)}, bf16[4096,1024]{1,0:T(8,128)(2,1)}, u32[]{:S(2)}) %copy-start) | copy-done | bytes 8388632
  4.0 0.0 copy-start.1
  4.0 1.6 %copy-done.1 = bf16[256,4096]{1,0:T(8,128)(2,1)S(1)} copy-done((bf16[256,4096]{1,0:T(8,128)(2,1)S(1)}, bf16[256,4096]{1,0:T(8,128)(2,1)}, u32[]{:S(2)}) %copy-start.1) | copy-done | bytes 2097176
  5.6 0.0 copy-start.2
  5.6 1.0 %copy-done.2 = bf16[256,1024]{1,0:T(8,128)(2,1)S(1)} copy-done((bf16[256,1024]{1,0:T(8,128)(2,1)S(1)}, bf16[256,1024]{1,0:T(8,128)(2,1)}, u32[]{:S(2)}) %copy-start.2) | copy-done | bytes 524312
  6.6 0.0 copy-start.3
  6.6 0.8 %copy-done.3 = bf16[1024,32]{0,1:T(8,128)(2,1)S(1)} copy-done((bf16[1024,32]{0,1:T(8,128)(2,1)S(1)}, bf16[1024,32]{0,1:T(8,128)(2,1)}, u32[]{:S(2)}) %copy-start.3) | copy-done | bytes 65560
  7.5 45.7 %powersgd_round.1 = (f32[32,4096]{1,0:T(8,128)S(1)}, f32[32,1024]{1,0:T(8,128)S(1)}) custom-call(bf16[256,4096]{1,0:T(8,128)(2,1)S(1)} %copy-done.1, bf16[256,1024]{1,0:T(8,128)(2,1)S(1)} %copy-done.2, bf16[4096,1024]{1,0:T(8,128)(2,1)S(1)} %copy-done, bf16[32,1024]{1,0:T(8,128)(2,1)S(1)} %bitcast.3), custom_call_target="tpu_custom_call" | custom-call | tf_op jit(solution)/shard_map/powersgd_round/pallas_call | solution.py:259
  53.2 6.2 %powersgd_update.1 = (bf16[4096,1024]{1,0:T(8,128)(2,1)}, f32[32,4096]{1,0:T(8,128)}, f32[32,1024]{1,0:T(8,128)}) custom-call(f32[32,4096]{1,0:T(8,128)S(1)} %get-tuple-element.8.basis, f32[32,1024]{1,0:T(8,128)S(1)} %get-tuple-element.9.coeff), custom_call_target="tpu_custom_call" | custom-call | tf_op jit(solution)/shard_map/powersgd_update/pallas_call | solution.py:287
Async XLA Ops:
  0.6 3.4 %copy-start = (bf16[4096,1024]{1,0:T(8,128)(2,1)S(1)}, bf16[4096,1024]{1,0:T(8,128)(2,1)}, u32[]{:S(2)}) copy-start(bf16[4096,1024]{1,0:T(8,128)(2,1)} %resid.1) | copy-start | bytes 25165828
  4.0 1.6 %copy-start.1 = (bf16[256,4096]{1,0:T(8,128)(2,1)S(1)}, bf16[256,4096]{1,0:T(8,128)(2,1)}, u32[]{:S(2)}) copy-start(bf16[256,4096]{1,0:T(8,128)(2,1)} %act.1) | copy-start | bytes 6291460
  5.6 1.0 %copy-start.2 = (bf16[256,1024]{1,0:T(8,128)(2,1)S(1)}, bf16[256,1024]{1,0:T(8,128)(2,1)}, u32[]{:S(2)}) copy-start(bf16[256,1024]{1,0:T(8,128)(2,1)} %grads.1) | copy-start | bytes 1572868
  6.6 0.8 %copy-start.3 = (bf16[1024,32]{0,1:T(8,128)(2,1)S(1)}, bf16[1024,32]{0,1:T(8,128)(2,1)}, u32[]{:S(2)}) copy-start(bf16[1024,32]{0,1:T(8,128)(2,1)} %param.7) | copy-start | bytes 196612

commit v2 on v1

v2 whole, which is shorter than its diff:
```python
import functools
import itertools

import jax
import jax.numpy as jnp
from jax import lax
from jax.experimental import pallas as pl
from jax.experimental.pallas import tpu as pltpu
from jax.sharding import PartitionSpec as P

LANES = 128
ROWS = 8
HIGHEST = lax.Precision.HIGHEST


def plain_shards(activations, out_grads, residual, right_prev):
    product = lax.dot_general(
        activations, out_grads, (((0,), (0,)), ((), ())), preferred_element_type=jnp.float32
    )
    merged = (product + residual.astype(jnp.float32)).astype(jnp.bfloat16)
    shard_sum = lax.psum_scatter(
        jnp.dot(merged, right_prev, preferred_element_type=jnp.float32),
        "tp",
        scatter_dimension=0,
        tiled=True,
    )
    block_sum = lax.psum(shard_sum, "dp")
    block_gram = jnp.dot(block_sum.T, block_sum, precision=HIGHEST)
    gram_matrix = lax.psum(block_gram, "tp")
    lower_factor = jnp.linalg.cholesky(gram_matrix)
    basis_block = lax.linalg.triangular_solve(
        lower_factor, block_sum, left_side=False, lower=True, transpose_a=True
    )
    left_basis = lax.all_gather(basis_block, "tp", axis=0, tiled=True)
    left_half = left_basis.astype(jnp.bfloat16)
    coeff_terms = lax.dot_general(
        merged, left_half, (((0,), (0,)), ((), ())), preferred_element_type=jnp.float32
    )
    right_factor = lax.psum(coeff_terms, "dp") / lax.axis_size("dp")
    update = jnp.dot(left_basis, right_factor.T, precision=HIGHEST).astype(jnp.bfloat16)
    return (update, left_basis, right_factor)


def digits_of(axis, size):
    if size == 1:
        return []
    if size % 2 == 0 and size > 2:
        return [(axis, 1, 2), (axis, 2, size // 2)]
    return [(axis, 1, size)]


def members(stage):
    count = 1
    for _, _, size in stage:
        count *= size
    return count


def offsets(stage):
    return list(itertools.product(*[range(size) for _, _, size in stage]))[1:]


def member_index(stage, place):
    index = 0
    for axis, stride, size in stage:
        index = index * size + (place[axis] // stride) % size
    return index


def moved(stage, offset, place, sign=1):
    there = dict(place)
    for (axis, stride, size), step in zip(stage, offset):
        digit = (place[axis] // stride) % size
        there[axis] = there[axis] + (((digit + sign * step + size) % size) - digit) * stride
    return there


def split(value):
    high = value.astype(jnp.bfloat16)
    return high, (value - high.astype(jnp.float32)).astype(jnp.bfloat16)


def joined(units, rank):
    tall = rank // ROWS
    n = units.shape[0] // tall
    bands = [
        jnp.concatenate([units[b * tall + r] for b in range(n)], axis=1) for r in range(tall)
    ]
    return jnp.concatenate(bands, axis=0)


def round_kernel(
    left_stages, right_stages, n_chunk, axes,
    act, grads, resid, right_prev, basis_out, coeff_out,
    xbuf, ybuf, rbuf, merged, terms, acc2, full2, *rest,
):
    rest = list(rest)
    in_sem, send_sem, recv_sem = rest[-3:]
    take = iter(rest[:-3])
    acc, full = next(take), next(take)
    left_recv = [next(take) for _ in left_stages]
    right_recv = [next(take) for _ in right_stages]
    place = {axis: lax.axis_index(axis) for axis in axes}
    barrier = pltpu.get_barrier_semaphore()
    peers = {}
    for stage in left_stages + right_stages:
        for offset in offsets(stage):
            key = tuple(sorted((d, s) for d, s in zip(stage, offset) if s))
            peers[key] = moved(stage, offset, place)
    for peer in peers.values():
        pl.semaphore_signal(barrier, inc=1, device_id=peer, device_id_type=pl.DeviceIdType.MESH)

    rows, columns = resid.shape
    rank = right_prev.shape[0]
    tall = rank // ROWS
    chunk = rows // n_chunk
    per = chunk // LANES
    units = per * tall
    first, second = left_stages[:2]
    n0, n1 = members(first), members(second)
    order = []
    for offset in offsets(first) + [(0,) * len(first)]:
        for offset2 in offsets(second) + [(0,) * len(second)]:
            there = moved(second, offset2, moved(first, offset, place))
            order.append(member_index(first, there) * n1 + member_index(second, there))

    def x_copy(c):
        at = pl.multiple_of(c * chunk, chunk)
        return pltpu.make_async_copy(act.at[:, pl.ds(at, chunk)], xbuf.at[c], in_sem.at[c])

    def e_copy(c):
        at = pl.multiple_of(c * chunk, chunk)
        return pltpu.make_async_copy(
            resid.at[pl.ds(at, chunk), :], merged.at[pl.ds(at, chunk), :], in_sem.at[n_chunk + c]
        )

    y_copy = pltpu.make_async_copy(grads, ybuf, in_sem.at[2 * n_chunk])
    r_copy = pltpu.make_async_copy(right_prev, rbuf, in_sem.at[2 * n_chunk + 1])
    y_copy.start()
    r_copy.start()
    for c in order:
        x_copy(c).start()
        e_copy(c).start()
    y_copy.wait()
    r_copy.wait()

    slot = [0]
    sent = []

    def remote(src, dst, peer):
        n = slot[0]
        slot[0] += 1
        copy = pltpu.make_async_remote_copy(
            src_ref=src, dst_ref=dst, send_sem=send_sem.at[n], recv_sem=recv_sem.at[n],
            device_id=peer, device_id_type=pl.DeviceIdType.MESH,
        )
        copy.start()
        sent.append(copy)
        return copy

    def all_reduce(stages, acc_ref, recv_refs, full_ref, lo, count, held):
        for stage, recv in zip(stages, recv_refs):
            size = count // members(stage)
            copies = []
            for k, offset in enumerate(offsets(stage)):
                peer = moved(stage, offset, place)
                start = lo + member_index(stage, peer) * size
                copies.append(remote(acc_ref.at[pl.ds(start, size)], recv.at[k], peer))
            held = held + [(stage, lo, count)]
            lo, count = lo + member_index(stage, place) * size, size
            yield
            total = acc_ref[pl.ds(lo, count)]
            for k, copy in enumerate(copies):
                copy.wait_recv()
                total = total + recv[k]
            if stage is stages[-1]:
                full_ref[pl.ds(lo, count)] = total
            else:
                acc_ref[pl.ds(lo, count)] = total
        for stage, outer, outer_count in reversed(held):
            copies = []
            for offset in offsets(stage):
                peer = moved(stage, offset, place)
                mine = full_ref.at[pl.ds(lo, count)]
                copies.append(remote(mine, mine, peer))
            yield
            for copy in copies:
                copy.wait_recv()
            lo, count = outer, outer_count

    def advance(flow):
        return next(flow, "done") != "done"

    def merge(c):
        x_copy(c).wait()
        e_copy(c).wait()
        at = pl.multiple_of(c * chunk, chunk)
        product = lax.dot_general(
            xbuf[c], ybuf[...], (((0,), (0,)), ((), ())), preferred_element_type=jnp.float32
        )
        piece = (product + merged[pl.ds(at, chunk), :].astype(jnp.float32)).astype(jnp.bfloat16)
        merged[pl.ds(at, chunk), :] = piece
        term = lax.dot_general(
            rbuf[...], piece, (((1,), (1,)), ((), ())), preferred_element_type=jnp.float32
        )
        return [
            term[r * ROWS : (r + 1) * ROWS, b * LANES : (b + 1) * LANES]
            for b in range(per) for r in range(tall)
        ]

    arrivals = {}
    second_copies = []
    for n, c in enumerate(order):
        k0, k1 = divmod(n, n1)
        terms_of_chunk = merge(c)
        at = c * units
        if n == 0:
            pl.semaphore_wait(barrier, len(peers))
        if k0 < n0 - 1:
            for u, term in enumerate(terms_of_chunk):
                acc[at + u] = term
            peer = moved(first, offsets(first)[k0], place)
            arrivals[k0, k1] = remote(acc.at[pl.ds(at, units)], left_recv[0].at[k0, k1], peer)
            continue
        for j in range(n0 - 1):
            arrivals[j, k1].wait_recv()
        for u, term in enumerate(terms_of_chunk):
            for j in range(n0 - 1):
                term = term + left_recv[0][j, k1, u]
            acc[at + u] = term
        if k1 < n1 - 1:
            peer = moved(second, offsets(second)[k1], place)
            second_copies.append(remote(acc.at[pl.ds(at, units)], left_recv[1].at[k1], peer))
    mine = order[-1] * units
    total = acc[pl.ds(mine, units)]
    for k, copy in enumerate(second_copies):
        copy.wait_recv()
        total = total + left_recv[1][k]
    acc[pl.ds(mine, units)] = total

    tile = 2 * LANES
    span = rows // n0

    def add_terms(index, step):
        at = pl.multiple_of(index * span, span)
        both = jnp.concatenate(
            split(joined(full[pl.ds(index * n1 * units, n1 * units)], rank)), axis=0
        )

        def column_tile(j, carry):
            col = pl.multiple_of(j * tile, tile)
            part = jnp.dot(
                both, merged[pl.ds(at, span), pl.ds(col, tile)],
                preferred_element_type=jnp.float32,
            )
            part = part[:rank] + part[rank:]
            if step > 0:
                part = part + terms[:, pl.ds(col, tile)]
            if step < n0 - 1:
                terms[:, pl.ds(col, tile)] = part
            else:
                for b in range(2):
                    for r in range(tall):
                        acc2[(2 * j + b) * tall + r] = part[
                            r * ROWS : (r + 1) * ROWS, b * LANES : (b + 1) * LANES
                        ]
            return carry

        lax.fori_loop(0, columns // tile, column_tile, 0)

    flow = all_reduce(
        left_stages[2:], acc, left_recv[2:], full, mine, units,
        [(first, 0, n_chunk * units), (second, member_index(first, place) * n1 * units, n1 * units)],
    )
    for _ in range(2 * len(left_stages[2:]) + 2):
        advance(flow)
    add_terms(member_index(first, place), 0)
    while advance(flow):
        pass
    for k, offset in enumerate(offsets(first)):
        add_terms(member_index(first, moved(first, offset, place)), k + 1)

    right_flow = all_reduce(right_stages, acc2, right_recv, full2, 0, acc2.shape[0], [])
    advance(right_flow)
    left_sum = joined(full[...], rank)
    gram = lax.dot_general(
        left_sum, left_sum, (((1,), (1,)), ((), ())),
        precision=HIGHEST, preferred_element_type=jnp.float32,
    )
    row_id = lax.broadcasted_iota(jnp.int32, (rank, LANES), 0)
    col_id = lax.broadcasted_iota(jnp.int32, (rank, LANES), 1)
    work = jnp.concatenate(
        [gram, (row_id + rank == col_id).astype(jnp.float32)[:, rank:]], axis=1
    )
    for j in range(rank):
        column = jnp.broadcast_to(work[:, j : j + 1], (rank, LANES))
        scaled = work[j : j + 1, :] / column[j : j + 1, :]
        work = work - jnp.where(row_id > j, column, 0.0) * scaled
    pivots = jnp.sum(jnp.where(row_id == col_id, work, 0.0), axis=1, keepdims=True)
    inverse = work[:, rank : 2 * rank] / jnp.sqrt(pivots)
    advance(right_flow)
    basis_out[...] = jnp.dot(
        inverse, left_sum, precision=HIGHEST, preferred_element_type=jnp.float32
    )
    while advance(right_flow):
        pass
    coeff_out[...] = jnp.dot(
        inverse * (1.0 / lax.axis_size("dp")), joined(full2[...], rank),
        precision=HIGHEST, preferred_element_type=jnp.float32,
    )
    for copy in sent:
        copy.wait_send()


def update_kernel(basis, coeff, update_out, basis_out, coeff_out):
    left_high, left_low = split(basis[...])
    right_high, right_low = split(coeff[...])
    left = jnp.concatenate([left_high, left_low, left_high], axis=0)
    right = jnp.concatenate([right_high, right_high, right_low], axis=0)
    update_out[...] = lax.dot_general(
        left, right, (((0,), (0,)), ((), ())), preferred_element_type=jnp.float32
    ).astype(jnp.bfloat16)
    basis_out[...] = basis[...]
    coeff_out[...] = coeff[...]


def fast_shards(axes, sizes, activations, out_grads, residual, right_prev):
    rows, columns = residual.shape
    tokens = activations.shape[0]
    rank = right_prev.shape[1]
    n_dp, n_tp = sizes["dp"], sizes["tp"]
    tp_digits, dp_digits = digits_of("tp", n_tp), digits_of("dp", n_dp)
    left_stages = [s for s in (tp_digits[:1], tp_digits[1:] + dp_digits[:1], dp_digits[1:]) if s]
    right_stages = [dp_digits]
    n_first, n_second = members(left_stages[0]), members(left_stages[1])
    n_chunk = n_first * n_second
    tall = rank // ROWS
    units, units2 = rows // LANES * tall, columns // LANES * tall

    def unit_buffer(*lead):
        return pltpu.VMEM((*lead, ROWS, LANES), jnp.float32)

    def recv_buffers(stages, count):
        buffers = []
        for stage in stages:
            count //= members(stage)
            buffers.append(unit_buffer(members(stage) - 1, count))
        return buffers

    n_copies = 2 * sum(members(s) - 1 for s in right_stages + left_stages[1:])
    n_copies += (n_first - 1) * (n_second + 1)
    vmem = pl.BlockSpec(memory_space=pltpu.VMEM)
    hbm = pl.BlockSpec(memory_space=pltpu.HBM)
    basis, coeff = pl.pallas_call(
        functools.partial(round_kernel, left_stages, right_stages, n_chunk, axes),
        out_shape=(
            jax.ShapeDtypeStruct((rank, rows), jnp.float32),
            jax.ShapeDtypeStruct((rank, columns), jnp.float32),
        ),
        in_specs=[hbm, hbm, hbm, hbm],
        out_specs=(vmem, vmem),
        scratch_shapes=[
            pltpu.VMEM((n_chunk, tokens, rows // n_chunk), jnp.bfloat16),
            pltpu.VMEM((tokens, columns), jnp.bfloat16),
            pltpu.VMEM((rank, columns), jnp.bfloat16),
            pltpu.VMEM((rows, columns), jnp.bfloat16),
            pltpu.VMEM((rank, columns), jnp.float32),
            unit_buffer(units2),
            unit_buffer(units2),
            unit_buffer(units),
            unit_buffer(units),
            unit_buffer(n_first - 1, n_second, units // n_chunk),
            *recv_buffers(left_stages[1:], units // n_first),
            *recv_buffers(right_stages, units2),
            pltpu.SemaphoreType.DMA((2 * n_chunk + 2,)),
            pltpu.SemaphoreType.DMA((n_copies,)),
            pltpu.SemaphoreType.DMA((n_copies,)),
        ],
        compiler_params=pltpu.CompilerParams(
            collective_id=0, has_side_effects=True, vmem_limit_bytes=63 * 2**20 + 512 * 2**10
        ),
        name="powersgd_round",
    )(activations, out_grads, residual, right_prev.T)
    step = rows // 4
    update, basis, coeff = pl.pallas_call(
        update_kernel,
        grid=(rows // step,),
        out_shape=(
            jax.ShapeDtypeStruct((rows, columns), jnp.bfloat16),
            jax.ShapeDtypeStruct((rank, rows), jnp.float32),
            jax.ShapeDtypeStruct((rank, columns), jnp.float32),
        ),
        in_specs=[
            pl.BlockSpec((rank, step), lambda i: (0, i)),
            pl.BlockSpec((rank, columns), lambda i: (0, 0)),
        ],
        out_specs=(
            pl.BlockSpec((step, columns), lambda i: (i, 0)),
            pl.BlockSpec((rank, step), lambda i: (0, i)),
            pl.BlockSpec((rank, columns), lambda i: (0, 0)),
        ),
        compiler_params=pltpu.CompilerParams(vmem_limit_bytes=16 * 2**20),
        name="powersgd_update",
    )(basis, coeff)
    return update, basis.T, coeff.T


def shards(axes, sizes, activations, out_grads, residual, right_prev):
    rows, columns = residual.shape
    rank = right_prev.shape[1]
    n_dp, n_tp = sizes["dp"], sizes["tp"]
    fits = (
        rank % ROWS == 0
        and 2 * rank <= LANES
        and min(n_dp, n_tp) > 1
        and n_dp % 2 == n_tp % 2 == 0
        and n_dp > 2
        and rows % (LANES * n_dp * n_tp) == 0
        and columns % (2 * LANES) == 0
        and (columns // LANES * (rank // ROWS)) % n_dp == 0
    )
    if not fits:
        return plain_shards(activations, out_grads, residual, right_prev)
    return fast_shards(axes, sizes, activations, out_grads, residual, right_prev)


def solution(mesh):
    in_specs = (P("dp", None), P("dp", "tp"), P("dp", "tp"), P("tp", None))
    out_specs = (P(None, "tp"), P(), P("tp", None))
    body = functools.partial(shards, mesh.axis_names, dict(mesh.shape))
    return jax.shard_map(body, mesh=mesh, in_specs=in_specs, out_specs=out_specs, check_vma=False)
```

time: 59.7 us -> 48.7 us (0.82)
  Pallas kernels: 51.9 us -> 45.9 us
  local copies, waits for them, and re-layouts: 6.85 us -> 1.94 us
    unnamed x8 -> x4, local copies, waits for them, and re-layouts: 6.85 us -> 1.94 us
    pallas_call x1, Pallas kernels: 45.7 us -> 41 us  [fast_shards(): pl.pallas_call(functools.partial(round_kernel, left_stages, right_stages,...]
    pallas_call x1, Pallas kernels: 6.25 us -> 4.92 us  [fast_shards(): pl.pallas_call(update_kernel, grid=(rows // step,), out_shape=(jax.ShapeD...]
where the time goes in v2:
time: 48.7 us; the launch traced here: 48.5 us
  Pallas kernels  45.9 us (94%)
  local copies, waits for them, and re-layouts  1.94 us (4%)
  between operations  0.65 us (1%)
    pallas_call x1, Pallas kernels, fast_shards(): pl.pallas_call(functools.partial(round_kernel, left_stages, right_stages,...  41 us
    pallas_call x1, Pallas kernels, fast_shards(): pl.pallas_call(update_kernel, grid=(rows // step,), out_shape=(jax.ShapeD...  4.92 us
    unnamed x4, local copies, waits for them, and re-layouts  1.94 us

profile of v2, /device:TPU:0, one launch (start us, length us, event | category | flops | bytes accessed | tf_op | source)
XLA Modules:
  0.0 48.5 jit_solution(1851627690144837218)
XLA Ops:
  0.6 41.0 %powersgd_round.1 = (f32[32,4096]{1,0:T(8,128)}, f32[32,1024]{1,0:T(8,128)}) custom-call(bf16[256,4096]{1,0:T(8,128)(2,1)} %act.1, bf16[256,1024]{1,0:T(8,128)(2,1)} %grads.1, bf16[4096,1024]{1,0:T(8,128)(2,1)} %resid.1, bf16[32,1024]{1,0:T(8,128)(2,1)} %bitcast.3), custom_call_target="tpu_custom_call" | custom-call | tf_op jit(solution)/shard_map/powersgd_round/pallas_call | solution.py:354
  41.6 0.0 copy-start
  41.6 1.0 %copy-done = f32[32,4096]{1,0:T(8,128)S(1)} copy-done((f32[32,4096]{1,0:T(8,128)S(1)}, f32[32,4096]{1,0:T(8,128)}, u32[]{:S(2)}) %copy-start) | copy-done | bytes 524312
  42.7 0.0 copy-start.1
  42.7 0.9 %copy-done.1 = f32[32,1024]{1,0:T(8,128)S(1)} copy-done((f32[32,1024]{1,0:T(8,128)S(1)}, f32[32,1024]{1,0:T(8,128)}, u32[]{:S(2)}) %copy-start.1) | copy-done | bytes 131096
  43.6 4.9 %powersgd_update.1 = (bf16[4096,1024]{1,0:T(8,128)(2,1)}, f32[32,4096]{1,0:T(8,128)}, f32[32,1024]{1,0:T(8,128)}) custom-call(f32[32,4096]{1,0:T(8,128)S(1)} %copy-done, f32[32,1024]{1,0:T(8,128)S(1)} %copy-done.1), custom_call_target="tpu_custom_call" | custom-call | tf_op jit(solution)/shard_map/powersgd_update/pallas_call | solution.py:385
Async XLA Ops:
  41.6 1.0 %copy-start = (f32[32,4096]{1,0:T(8,128)S(1)}, f32[32,4096]{1,0:T(8,128)}, u32[]{:S(2)}) copy-start(f32[32,4096]{1,0:T(8,128)} %get-tuple-element.8.basis) | copy-start | bytes 1572868
  42.7 0.9 %copy-start.1 = (f32[32,1024]{1,0:T(8,128)S(1)}, f32[32,1024]{1,0:T(8,128)}, u32[]{:S(2)}) copy-start(f32[32,1024]{1,0:T(8,128)} %get-tuple-element.9.coeff) | copy-start | bytes 393220

commit v3 on v2

--- a/solution.py
+++ b/solution.py
@@ -399,7 +399,7 @@
             pl.BlockSpec((rank, step), lambda i: (0, i)),
             pl.BlockSpec((rank, columns), lambda i: (0, 0)),
         ),
-        compiler_params=pltpu.CompilerParams(vmem_limit_bytes=16 * 2**20),
+        compiler_params=pltpu.CompilerParams(vmem_limit_bytes=63 * 2**20 + 512 * 2**10),
         name="powersgd_update",
     )(basis, coeff)
     return update, basis.T, coeff.T

time: 48.7 us -> 47.9 us (0.984)
  local copies, waits for them, and re-layouts: 1.94 us -> 0 us
  Pallas kernels: 45.9 us -> 47.1 us
    unnamed x4 -> x0, local copies, waits for them, and re-layouts: 1.94 us -> none
    pallas_call x1, Pallas kernels: 4.92 us -> 6.15 us  [fast_shards(): pl.pallas_call(update_kernel, grid=(rows // step,), out_shape=(jax.ShapeD...]
where the time goes in v3:
time: 47.9 us; the launch traced here: 47.8 us
  Pallas kernels  47.1 us (98%)
  between operations  0.64 us (1%)
    pallas_call x1, Pallas kernels, fast_shards(): pl.pallas_call(functools.partial(round_kernel, left_stages, right_stages,...  41 us
    pallas_call x1, Pallas kernels, fast_shards(): pl.pallas_call(update_kernel, grid=(rows // step,), out_shape=(jax.ShapeD...  6.15 us

profile of v3, /device:TPU:0, one launch (start us, length us, event | category | flops | bytes accessed | tf_op | source)
XLA Modules:
  0.0 47.8 jit_solution(7382722826912837022)
XLA Ops:
  0.6 41.0 %powersgd_round.1 = (f32[32,4096]{1,0:T(8,128)}, f32[32,1024]{1,0:T(8,128)}) custom-call(bf16[256,4096]{1,0:T(8,128)(2,1)} %act.1, bf16[256,1024]{1,0:T(8,128)(2,1)} %grads.1, bf16[4096,1024]{1,0:T(8,128)(2,1)} %resid.1, bf16[32,1024]{1,0:T(8,128)(2,1)} %bitcast.3), custom_call_target="tpu_custom_call" | custom-call | tf_op jit(solution)/shard_map/powersgd_round/pallas_call | solution.py:354
  41.6 6.2 %powersgd_update.1 = (bf16[4096,1024]{1,0:T(8,128)(2,1)}, f32[32,4096]{1,0:T(8,128)}, f32[32,1024]{1,0:T(8,128)}) custom-call(f32[32,4096]{1,0:T(8,128)} %get-tuple-element.8.basis, f32[32,1024]{1,0:T(8,128)} %get-tuple-element.9.coeff), custom_call_target="tpu_custom_call" | custom-call | tf_op jit(solution)/shard_map/powersgd_update/pallas_call | solution.py:385
